TPU v7x, 128 devices: a whole 4x4x4 slice. The times are simulated.
128 devices in a mesh: animal: 16 (over z, x_lo, core), snp: 8 (over x_hi, y).
Axes of the slice: x: 4 (x_hi: 2, x_lo: 2; x = x_hi * 2 + x_lo), y: 4, z: 4, core: 2. Of those that a mesh axis runs over, the one named last changes fastest.
Arguments:
- genotypes: int32 [32768, 8192], P('animal', 'snp'), may hold values from 0 to 2730, as said below
- allele_frequency: float32 [49152], P('snp'), may hold values from 0.05 to 0.5
- family_size: int32 [256], P('animal'), may hold values from 40 to 128, as said below
- rel_family: int32 [256], P('animal'), may hold values from 0 to 255, as said below
- rel_count: int32 [256], P('animal'), may hold values from 8 to 128, as said below
- own_block: bfloat16 [256, 128, 128], P('animal'), may hold values from -0.5 to 3
- rel_block: bfloat16 [256, 128, 128], P('animal'), may hold values from -0.5 to 0.5
- prior_solution: bfloat16 [32768, 128], P('animal'), may hold values from -6 to 6
- right_side: float32 [32768, 128], P('animal'), may hold values from -6 to 6
- step_scale: float32 [32768], P('animal'), may hold values from 0.1 to 0.3
Outputs:
- solution: float32 [32768, 128], P(('animal', 'snp'))
- residual: float32 [32768, 128], P(('animal', 'snp'))
Inputs may be any that keep to these rules, and one draw needn't show every extreme that they name: `genotypes`: bits 2k and 2k + 1 of word w of a row hold the code 0, 1 or 2 of marker 6w + k, for k = 0 to 5; higher bits are zero; some word has all six codes 0 and some word all six codes 2. `family_size`: some family has all 128 slots live. `rel_family`: family f's relative family lies in the same block of 16 consecutive families as f or in one of the 3 blocks before it, and in the block exactly 3 before it for some family of every block that has one. `rel_count`: some family takes all 128 rows.
All inputs are finite; a program needn't handle non-finite values.
Results may differ from a plain program's by a relative error of at most 0.007.
Values may be sent and summed in bfloat16 or wider, within the bound.
A program may use at most 192 MiB of HBM per device.

v0:
```python
import jax
import jax.numpy as jnp
from jax import lax
from jax.sharding import PartitionSpec as P

SNPS = 49152
ITERS = 2
RSPAN = 3


GEN_WEIGHT = 6.0


def shifted(array, axis, by):
    count = lax.axis_size(axis)
    pairs = [(i, i + by) for i in range(count) if 0 <= i + by < count]
    return lax.ppermute(array, axis, pairs)


def in_blocks(array, dim, count):
    before, after = (array.shape[:dim], array.shape[dim + 1 :])
    return jnp.moveaxis(array.reshape(*before, count, -1, *after), dim, 0)


def sum_at_owner(array, axis, dim):
    tiles = in_blocks(array, dim, lax.axis_size(axis))
    arrived = lax.all_to_all(tiles, axis, split_axis=0, concat_axis=0, tiled=True)
    return arrived.sum(axis=0)


def copy_for_each(array, axis):
    copies = jnp.broadcast_to(array, (lax.axis_size(axis), *array.shape))
    return lax.all_to_all(copies, axis, split_axis=0, concat_axis=0, tiled=True)


def joined_along(tiles, dim):
    lengths = list(tiles.shape[1:])
    lengths[dim] *= tiles.shape[0]
    return jnp.moveaxis(tiles, 0, dim).reshape(lengths)


def gathered_copies(array, axis, dim):
    tiles = copy_for_each(array, axis)
    return joined_along(tiles, dim)


def decode_rows(genotypes, allele_frequency, live_rows):
    bit_shifts = 2 * jnp.arange(6, dtype=jnp.int32)
    dosage_states = jnp.bitwise_and(
        jnp.right_shift(genotypes[:, :, None], bit_shifts[None, None, :]), 3
    )
    dosage_states = dosage_states.reshape(genotypes.shape[0], genotypes.shape[1] * 6).astype(
        jnp.float32
    )
    centered = (dosage_states - 2.0 * allele_frequency[None, :]) * live_rows[:, None]
    return centered.astype(jnp.bfloat16)


def decode_blocks(genotypes, allele_frequency, live_rows, family_count, block_order):
    group_count = family_count // 4
    group_rows = 4 * block_order
    packed_marker_groups = genotypes.reshape(group_count, group_rows, genotypes.shape[1])
    live_groups = live_rows.reshape(group_count, group_rows)

    def decode_group(inputs):
        return decode_rows(inputs[0], allele_frequency, inputs[1])

    decoded = lax.map(decode_group, (packed_marker_groups, live_groups))
    return decoded.reshape(family_count * block_order, genotypes.shape[1] * 6)


def live_mask(family_size, block_order):
    slot_index = jnp.arange(block_order, dtype=jnp.int32)
    return (slot_index[None, :] < family_size[:, None]).astype(jnp.float32).reshape(-1)


def mask_rows(relatives, rel_count, block_order):
    keep_rows = jnp.arange(block_order, dtype=jnp.int32)[None, :, None] < rel_count[:, None, None]
    return jnp.where(keep_rows, relatives, jnp.zeros_like(relatives))


def fetch_relatives(solution_half, rel_family, rel_count, family_count, block_order, columns):
    lower_blocks = [solution_half]
    for starting_displacement in range(1, RSPAN + 1):
        lower_blocks.append(shifted(solution_half, "animal", starting_displacement))
    stacked = jnp.stack(lower_blocks).reshape((RSPAN + 1) * family_count, block_order, columns)
    own_device = lax.axis_index("animal")
    distance = own_device - rel_family // family_count
    position = distance * family_count + rel_family % family_count
    relatives = jnp.take(stacked, position, axis=0)
    return mask_rows(relatives, rel_count, block_order)


def pedigree_term(own_block, rel_block, own_half, relatives):
    first_part = jnp.einsum("fij,fjk->fik", own_block, own_half, preferred_element_type=jnp.float32)
    return first_part + jnp.einsum(
        "fij,fjk->fik", rel_block, relatives, preferred_element_type=jnp.float32
    )


def per_device(
    genotypes,
    allele_frequency,
    family_size,
    rel_family,
    rel_count,
    own_block,
    rel_block,
    prior_solution,
    right_side,
    step_scale,
):
    family_count = own_block.shape[0]
    block_order = own_block.shape[1]
    columns = prior_solution.shape[1]
    row_count = family_count * block_order
    live_rows = live_mask(family_size, block_order)
    centered = decode_blocks(genotypes, allele_frequency, live_rows, family_count, block_order)
    share_families = family_count // lax.axis_size("snp")
    share_rows = share_families * block_order
    share_position = lax.axis_index("snp")
    family_first = share_position * share_families
    row_first = share_position * share_rows
    relative_part = lax.dynamic_slice_in_dim(rel_family, family_first, share_families, 0)
    count_part = lax.dynamic_slice_in_dim(rel_count, family_first, share_families, 0)
    solution_now = live_rows[:, None] * prior_solution.astype(jnp.float32)
    residual = jnp.zeros((row_count, columns), jnp.float32)
    for iteration in range(ITERS):
        solution_half = solution_now.astype(jnp.bfloat16)
        partial_sum = lax.dot_general(
            centered, solution_half, (((0,), (0,)), ((), ())), preferred_element_type=jnp.float32
        )
        snp_half = lax.psum(partial_sum, "animal").astype(jnp.bfloat16)
        genomic_part = jnp.dot(centered, snp_half, preferred_element_type=jnp.float32)
        relatives = fetch_relatives(
            solution_half, relative_part, count_part, family_count, block_order, columns
        )
        genomic = sum_at_owner(genomic_part, "snp", 0)
        own_part = lax.dynamic_slice_in_dim(own_block, family_first, share_families, 0)
        couple_part = lax.dynamic_slice_in_dim(rel_block, family_first, share_families, 0)
        own_half = lax.dynamic_slice_in_dim(solution_half, row_first, share_rows, 0).reshape(
            share_families, block_order, columns
        )
        pedigree = pedigree_term(own_part, couple_part, own_half, relatives).reshape(
            share_rows, columns
        )
        live_part = lax.dynamic_slice_in_dim(live_rows, row_first, share_rows, 0)
        right_part = lax.dynamic_slice_in_dim(right_side, row_first, share_rows, 0)
        scale_part = lax.dynamic_slice_in_dim(step_scale, row_first, share_rows, 0)
        solution_part = lax.dynamic_slice_in_dim(solution_now, row_first, share_rows, 0)
        residual = live_part[:, None] * (
            right_part - solution_part - GEN_WEIGHT / SNPS * genomic - pedigree
        )
        solution_part = solution_part + scale_part[:, None] * residual
        if iteration + 1 < ITERS:
            solution_now = gathered_copies(solution_part.astype(jnp.bfloat16), "snp", 0).astype(
                solution_part.dtype
            )
        else:
            solution_now = solution_part
    return (solution_now, residual)


def solution(mesh):
    in_specs = (
        P("animal", "snp"),
        P("snp"),
        P("animal"),
        P("animal"),
        P("animal"),
        P("animal", None, None),
        P("animal", None, None),
        P("animal", None),
        P("animal", None),
        P("animal"),
    )
    out_specs = (P(("animal", "snp"), None), P(("animal", "snp"), None))
    return jax.shard_map(
        per_device, mesh=mesh, in_specs=in_specs, out_specs=out_specs, check_vma=False
    )
```

profile of v0, /device:TPU:1, one launch (start us, length us, event | category | flops | bytes accessed | tf_op | source)
XLA Modules:
  0.0 507.8 jit_solution(6328784146243284202)
XLA Ops:
  16.4 210.8 %while.10 = (s32[]{:T(128)}, bf16[4,512,6144]{2,1,0:T(8,128)(2,1)}, s32[4,512,1024]{2,1,0:T(8,128)}, f32[6144]{0:T(1024)}, f32[4,512]{1,0:T(4,128)S(1)}, /*index=5*/s32[]{:T(128)}) while((s32[]{:T(128)}, bf16[4,512,6144]{2,1,0:T(8,128)(2,1)}, s32[4,512,1024]{2,1,0:T(8,128)}, f32[6144]{0:T(1024)}, f32[4,512]{1,0:T(4,128)S(1)}, ...), condition=%wide.region_1.2_spmd, body=%wide.region_0.1_spmd.sunk | while | flops 18880520 | bytes 92551832 | solution.py:68
  21.5 8.0 %shift_right_arithmetic.39 = s32[512,1024,6]{0,2,1:T(8,128)} broadcast(s32[512,1024]{0,1:T(8,128)S(1)} %bitcast.61), dimensions={0,1} | broadcast | bytes 14680064 | tf_op jit(solution)/shard_map/while/body/eval_jaxpr/shift_right_arithmetic | solution.py:50
  29.5 15.6 %shift_right_arithmetic.40 = s32[1,512,6144]{1,2,0:T(8,128)} reshape(s32[512,1024,6]{0,2,1:T(8,128)} %shift_right_arithmetic.39) | data formatting | bytes 25165824 | tf_op jit(solution)/shard_map/while/body/eval_jaxpr/shift_right_arithmetic | solution.py:50
  45.6 8.7 %multiply_convert_fusion.2 = bf16[1,512,6144]{1,2,0:T(8,128)(2,1)} fusion(s32[1,512,6144]{1,2,0:T(8,128)} %shift_right_arithmetic.40, f32[512]{0:T(512)S(1)} %bitcast.76, f32[6144]{0:T(1024)S(1)} %broadcast_multiply_fusion.2, s32[6144]{0:T(1024)S(1)} %shift_right_arithmetic.42), kind=kLoop, calls=%fused_computation.2.clone.1 | loop fusion | flops 18874368 | bytes 18925568 | tf_op jit(solution)/shard_map/while/body/eval_jaxpr/convert_element_type | solution.py:56
  54.3 8.7 %copy.25 = bf16[1,512,6144]{2,1,0:T(8,128)(2,1)} copy(bf16[1,512,6144]{1,2,0:T(8,128)(2,1)} %multiply_convert_fusion.2) | data formatting | bytes 12582912 | tf_op jit(solution)/shard_map/while/body/jit(dynamic_update_index_in_dim)/dynamic_update_slice | solution.py:68
  74.3 8.0 %shift_right_arithmetic.39 = s32[512,1024,6]{0,2,1:T(8,128)} broadcast(s32[512,1024]{0,1:T(8,128)S(1)} %bitcast.61), dimensions={0,1} | broadcast | bytes 14680064 | tf_op jit(solution)/shard_map/while/body/eval_jaxpr/shift_right_arithmetic | solution.py:50
  82.3 15.6 %shift_right_arithmetic.40 = s32[1,512,6144]{1,2,0:T(8,128)} reshape(s32[512,1024,6]{0,2,1:T(8,128)} %shift_right_arithmetic.39) | data formatting | bytes 25165824 | tf_op jit(solution)/shard_map/while/body/eval_jaxpr/shift_right_arithmetic | solution.py:50
  98.3 8.7 %multiply_convert_fusion.2 = bf16[1,512,6144]{1,2,0:T(8,128)(2,1)} fusion(s32[1,512,6144]{1,2,0:T(8,128)} %shift_right_arithmetic.40, f32[512]{0:T(512)S(1)} %bitcast.76, f32[6144]{0:T(1024)S(1)} %broadcast_multiply_fusion.2, s32[6144]{0:T(1024)S(1)} %shift_right_arithmetic.42), kind=kLoop, calls=%fused_computation.2.clone.1 | loop fusion | flops 18874368 | bytes 18925568 | tf_op jit(solution)/shard_map/while/body/eval_jaxpr/convert_element_type | solution.py:56
  107.0 8.7 %copy.25 = bf16[1,512,6144]{2,1,0:T(8,128)(2,1)} copy(bf16[1,512,6144]{1,2,0:T(8,128)(2,1)} %multiply_convert_fusion.2) | data formatting | bytes 12582912 | tf_op jit(solution)/shard_map/while/body/jit(dynamic_update_index_in_dim)/dynamic_update_slice | solution.py:68
  127.0 8.0 %shift_right_arithmetic.39 = s32[512,1024,6]{0,2,1:T(8,128)} broadcast(s32[512,1024]{0,1:T(8,128)S(1)} %bitcast.61), dimensions={0,1} | broadcast | bytes 14680064 | tf_op jit(solution)/shard_map/while/body/eval_jaxpr/shift_right_arithmetic | solution.py:50
  135.0 15.6 %shift_right_arithmetic.40 = s32[1,512,6144]{1,2,0:T(8,128)} reshape(s32[512,1024,6]{0,2,1:T(8,128)} %shift_right_arithmetic.39) | data formatting | bytes 25165824 | tf_op jit(solution)/shard_map/while/body/eval_jaxpr/shift_right_arithmetic | solution.py:50
  151.0 8.7 %multiply_convert_fusion.2 = bf16[1,512,6144]{1,2,0:T(8,128)(2,1)} fusion(s32[1,512,6144]{1,2,0:T(8,128)} %shift_right_arithmetic.40, f32[512]{0:T(512)S(1)} %bitcast.76, f32[6144]{0:T(1024)S(1)} %broadcast_multiply_fusion.2, s32[6144]{0:T(1024)S(1)} %shift_right_arithmetic.42), kind=kLoop, calls=%fused_computation.2.clone.1 | loop fusion | flops 18874368 | bytes 18925568 | tf_op jit(solution)/shard_map/while/body/eval_jaxpr/convert_element_type | solution.py:56
  159.7 8.7 %copy.25 = bf16[1,512,6144]{2,1,0:T(8,128)(2,1)} copy(bf16[1,512,6144]{1,2,0:T(8,128)(2,1)} %multiply_convert_fusion.2) | data formatting | bytes 12582912 | tf_op jit(solution)/shard_map/while/body/jit(dynamic_update_index_in_dim)/dynamic_update_slice | solution.py:68
  179.7 8.0 %shift_right_arithmetic.39 = s32[512,1024,6]{0,2,1:T(8,128)} broadcast(s32[512,1024]{0,1:T(8,128)S(1)} %bitcast.61), dimensions={0,1} | broadcast | bytes 14680064 | tf_op jit(solution)/shard_map/while/body/eval_jaxpr/shift_right_arithmetic | solution.py:50
  187.7 15.6 %shift_right_arithmetic.40 = s32[1,512,6144]{1,2,0:T(8,128)} reshape(s32[512,1024,6]{0,2,1:T(8,128)} %shift_right_arithmetic.39) | data formatting | bytes 25165824 | tf_op jit(solution)/shard_map/while/body/eval_jaxpr/shift_right_arithmetic | solution.py:50
  203.7 8.7 %multiply_convert_fusion.2 = bf16[1,512,6144]{1,2,0:T(8,128)(2,1)} fusion(s32[1,512,6144]{1,2,0:T(8,128)} %shift_right_arithmetic.40, f32[512]{0:T(512)S(1)} %bitcast.76, f32[6144]{0:T(1024)S(1)} %broadcast_multiply_fusion.2, s32[6144]{0:T(1024)S(1)} %shift_right_arithmetic.42), kind=kLoop, calls=%fused_computation.2.clone.1 | loop fusion | flops 18874368 | bytes 18925568 | tf_op jit(solution)/shard_map/while/body/eval_jaxpr/convert_element_type | solution.py:56
  212.4 8.7 %copy.25 = bf16[1,512,6144]{2,1,0:T(8,128)(2,1)} copy(bf16[1,512,6144]{1,2,0:T(8,128)(2,1)} %multiply_convert_fusion.2) | data formatting | bytes 12582912 | tf_op jit(solution)/shard_map/while/body/jit(dynamic_update_index_in_dim)/dynamic_update_slice | solution.py:68
  227.2 12.9 %fusion.39 = f32[6144,128]{1,0:T(8,128)} fusion(bf16[2048,6144]{1,0:T(8,128)(2,1)} %bitcast.77, bf16[2048,128]{1,0:T(8,128)(2,1)} %get-tuple-element.51), kind=kOutput, calls=%fused_computation.72 | convolution fusion | flops 3221225472 | bytes 28835840 | tf_op jit(solution)/shard_map/dot_general | solution.py:130
  240.1 77.1 %all-reduce.2 = bf16[6144,128]{1,0:T(8,128)(2,1)S(1)} all-reduce(f32[6144,128]{1,0:T(8,128)} %fusion.39), channel_id=1, replica_groups=mesh['animal'=16,'snp'=8] {'animal'}, use_global_device_ids=true, to_apply=%region_2.3 | all-reduce | flops 786432 | bytes 4718592 | tf_op jit(solution)/shard_map/psum | solution.py:133
  317.2 12.6 %fusion.2 = f32[8,256,128]{2,1,0:T(8,128)} fusion(bf16[8,256,6144]{2,1,0:T(8,128)(2,1)} %bitcast.78, bf16[6144,128]{1,0:T(8,128)(2,1)S(1)} %all-reduce.2), kind=kOutput, calls=%fused_computation.12 | convolution fusion | flops 3221225472 | bytes 27787264 | tf_op jit(solution)/shard_map/dot_general | solution.py:134
  349.7 16.4 %all_to_all.15 = bf16[8,256,128]{2,1,0:T(8,128)(2,1)S(1)} all-to-all(bf16[8,256,128]{2,1,0:T(8,128)(2,1)S(1)} %broadcast_in_dim.32), channel_id=1, replica_groups=mesh['animal'=16,'snp'=8] {'snp'}, dimensions={0} | all-to-all | bytes 1048576 | tf_op jit(solution)/shard_map/all_to_all | solution.py:33
  366.1 13.4 %fusion.40 = f32[6144,128]{1,0:T(8,128)} fusion(bf16[2048,6144]{1,0:T(8,128)(2,1)} %bitcast.79, bf16[2048,128]{1,0:T(8,128)(2,1)S(1)} %bitcast.63), kind=kOutput, calls=%fused_computation.73 | convolution fusion | flops 3221225472 | bytes 28835840 | tf_op jit(solution)/shard_map/dot_general | solution.py:130
  388.6 88.9 %all-reduce.3 = bf16[6144,128]{1,0:T(8,128)(2,1)} all-reduce(f32[6144,128]{1,0:T(8,128)} %fusion.40), channel_id=1, replica_groups=mesh['animal'=16,'snp'=8] {'animal'}, use_global_device_ids=true, to_apply=%region_4.6 | all-reduce | flops 786432 | bytes 4718592 | tf_op jit(solution)/shard_map/psum | solution.py:133
  477.4 12.9 %fusion = f32[8,256,128]{2,1,0:T(8,128)} fusion(bf16[8,256,6144]{2,1,0:T(8,128)(2,1)} %bitcast.80, bf16[6144,128]{1,0:T(8,128)(2,1)} %all-reduce.3), kind=kOutput, calls=%fused_computation.10 | convolution fusion | flops 3221225472 | bytes 27787264 | tf_op jit(solution)/shard_map/dot_general | solution.py:134
  (92 shorter events, 108.8 us)
Async XLA Ops:
  0.6 338.5 %copy-start = (bf16[16,128,128]{2,1,0:T(8,128)(2,1)S(1)}, bf16[16,128,128]{2,1,0:T(8,128)(2,1)}, u32[]{:S(2)}) copy-start(bf16[16,128,128]{2,1,0:T(8,128)(2,1)} %param.19) | copy-start | bytes 1572868
  1.4 0.6 copy-start.2
  4.6 334.7 %collective-permute-start = (bf16[2048,128]{1,0:T(8,128)(2,1)}, bf16[2048,128]{1,0:T(8,128)(2,1)}, u32[]{:S(2)}, u32[]{:S(2)}) collective-permute-start(bf16[2048,128]{1,0:T(8,128)(2,1)} %get-tuple-element.51), channel_id=1, source_target_pairs={{0,8},{8,16},{16,24},{24,32},{32,40},{40,48},{48,56},{56,64},{64,7... | collective-permute-start | bytes 1572872 | tf_op jit(solution)/shard_map/ppermute | solution.py:17
  9.0 330.2 %collective-permute-start.1 = (bf16[2048,128]{1,0:T(8,128)(2,1)}, bf16[2048,128]{1,0:T(8,128)(2,1)}, u32[]{:S(2)}, u32[]{:S(2)}) collective-permute-start(bf16[2048,128]{1,0:T(8,128)(2,1)} %get-tuple-element.51), channel_id=1, source_target_pairs={{0,16},{8,24},{16,32},{24,40},{32,48},{40,56},{48,64},{56,72},{64,... | collective-permute-start | bytes 1572872 | tf_op jit(solution)/shard_map/ppermute | solution.py:17
  13.4 325.9 %collective-permute-start.2 = (bf16[2048,128]{1,0:T(8,128)(2,1)}, bf16[2048,128]{1,0:T(8,128)(2,1)}, u32[]{:S(2)}, u32[]{:S(2)}) collective-permute-start(bf16[2048,128]{1,0:T(8,128)(2,1)} %get-tuple-element.51), channel_id=1, source_target_pairs={{0,24},{8,32},{16,40},{24,48},{32,56},{40,64},{48,72},{56,80},{64,... | collective-permute-start | bytes 1572872 | tf_op jit(solution)/shard_map/ppermute | solution.py:17
  29.5 15.6 %copy-start.1 = (f32[6144]{0:T(1024)S(1)}, f32[6144]{0:T(1024)}, u32[]{:S(2)}) copy-start(f32[6144]{0:T(1024)} %get-tuple-element.98) | copy-start | bytes 73732 | tf_op jit(solution)/shard_map/while
  82.3 15.6 %copy-start.1 = (f32[6144]{0:T(1024)S(1)}, f32[6144]{0:T(1024)}, u32[]{:S(2)}) copy-start(f32[6144]{0:T(1024)} %get-tuple-element.98) | copy-start | bytes 73732 | tf_op jit(solution)/shard_map/while
  135.0 15.6 %copy-start.1 = (f32[6144]{0:T(1024)S(1)}, f32[6144]{0:T(1024)}, u32[]{:S(2)}) copy-start(f32[6144]{0:T(1024)} %get-tuple-element.98) | copy-start | bytes 73732 | tf_op jit(solution)/shard_map/while
  187.7 15.6 %copy-start.1 = (f32[6144]{0:T(1024)S(1)}, f32[6144]{0:T(1024)}, u32[]{:S(2)}) copy-start(f32[6144]{0:T(1024)} %get-tuple-element.98) | copy-start | bytes 73732 | tf_op jit(solution)/shard_map/while
  317.2 21.6 %copy-start.4 = (s32[16]{0:T(128)S(1)}, s32[16]{0:T(128)}, u32[]{:S(2)}) copy-start(s32[16]{0:T(128)} %param.18) | copy-start | bytes 196
  317.2 21.7 %copy-start.3 = (s32[16]{0:T(128)S(1)}, s32[16]{0:T(128)}, u32[]{:S(2)}) copy-start(s32[16]{0:T(128)} %param.17) | copy-start | bytes 196
  329.8 18.6 %all-to-all-start = ((f32[8,256,128]{2,1,0:T(8,128)}), f32[8,256,128]{2,1,0:T(8,128)S(1)}, u32[]{:S(2)}, u32[]{:S(2)}) async-start(f32[8,256,128]{2,1,0:T(8,128)} %fusion.2), calls=%async_computation | async-start | bytes 2097152 | tf_op jit(solution)/shard_map/all_to_all | solution.py:27
  379.5 114.6 %collective-permute-start.3 = (bf16[2048,128]{1,0:T(8,128)(2,1)S(1)}, bf16[2048,128]{1,0:T(8,128)(2,1)S(1)}, u32[]{:S(2)}, u32[]{:S(2)}) collective-permute-start(bf16[2048,128]{1,0:T(8,128)(2,1)S(1)} %bitcast.64), channel_id=1, source_target_pairs={{0,8},{8,16},{16,24},{24,32},{32,40},{40,48},{48,56},{56,64},{64,7... | collective-permute-start | bytes 1572872 | tf_op jit(solution)/shard_map/ppermute | solution.py:17
  382.5 111.6 %collective-permute-start.4 = (bf16[2048,128]{1,0:T(8,128)(2,1)S(1)}, bf16[2048,128]{1,0:T(8,128)(2,1)S(1)}, u32[]{:S(2)}, u32[]{:S(2)}) collective-permute-start(bf16[2048,128]{1,0:T(8,128)(2,1)S(1)} %bitcast.65), channel_id=1, source_target_pairs={{0,16},{8,24},{16,32},{24,40},{32,48},{40,56},{48,64},{56,72},{64,... | collective-permute-start | bytes 1572872 | tf_op jit(solution)/shard_map/ppermute | solution.py:17
  384.9 109.1 %collective-permute-start.5 = (bf16[2048,128]{1,0:T(8,128)(2,1)S(1)}, bf16[2048,128]{1,0:T(8,128)(2,1)}, u32[]{:S(2)}, u32[]{:S(2)}) collective-permute-start(bf16[2048,128]{1,0:T(8,128)(2,1)S(1)} %bitcast.66), channel_id=1, source_target_pairs={{0,24},{8,32},{16,40},{24,48},{32,56},{40,64},{48,72},{56,80},{64,... | collective-permute-start | bytes 1572872 | tf_op jit(solution)/shard_map/ppermute | solution.py:17
  490.3 15.8 %all-to-all-start.2 = ((f32[8,256,128]{2,1,0:T(8,128)}), f32[8,256,128]{2,1,0:T(8,128)S(1)}, u32[]{:S(2)}, u32[]{:S(2)}) async-start(f32[8,256,128]{2,1,0:T(8,128)} %fusion), calls=%async_computation.2 | async-start | bytes 2097152 | tf_op jit(solution)/shard_map/all_to_all | solution.py:27
where the time goes:
time: 515 us; the launch traced here: 508 us
  local copies, waits for them, and re-layouts  184 us (36%)
  blocking collectives  182 us (35%)
  matrix products  54.2 us (11%)
  other arithmetic  47 us (9%)
  starting transfers between devices  30.3 us (6%)
  waiting for transfers between devices  8.87 us (2%)
    psum x2, blocking collectives, per_device(): snp_half = lax.psum(partial_sum, 'animal').astype(jnp.bfloat16)  166 us
    shift_right_arithmetic x16, local copies, waits for them, and re-layouts, decode_rows(): jnp.right_shift(genotypes[:, :, None], bit_shifts[None, None, :])  96 us
    dynamic_update_slice x8, local copies, waits for them, and re-layouts, decode_blocks(): decoded = lax.map(decode_group, (packed_marker_groups, live_groups))  59.4 us
    convert_element_type x4, other arithmetic, decode_rows(): return centered.astype(jnp.bfloat16)  34.7 us
    dot_general x2, matrix products, per_device(): lax.dot_general(centered, solution_half, (((0,), (0,)), ((), ())), prefer...  26.3 us
    dot_general x2, matrix products, per_device(): jnp.dot(centered, snp_half, preferred_element_type=jnp.float32)  25.4 us
    dynamic_slice x12, local copies, waits for them, and re-layouts, decode_blocks(): decoded = lax.map(decode_group, (packed_marker_groups, live_groups))  20.5 us
    ppermute x6, starting transfers between devices, shifted(): return lax.ppermute(array, axis, pairs)  20.1 us
  transfers between devices with their start and end apart: 8, of which 2 were waited for; matrix products, arithmetic and copies ran while one was open for 52% of the time, Pallas kernels for 0%

commit v1 on v0

v1 whole, which is shorter than its diff:
```python
import jax
import jax.numpy as jnp
from jax import lax
from jax.experimental import pallas as pl
from jax.experimental.pallas import tpu as pltpu
from jax.sharding import PartitionSpec as P

SNPS = 49152
ITERS = 2
RSPAN = 3
GEN_WEIGHT = 6.0
PLANES = 6
FAM = 128
COLS = 128
ANIMAL = 16
SNP = 8
CHIPS = 8
ROWS = 2048
WORDS = 1024
FAMS = 16
SHARE = 256
HALF = 512
BAND = 16
ROW_BLOCKS = 8

F32 = jnp.float32
BF16 = jnp.bfloat16


def dot(a, b, ca, cb):
    return lax.dot_general(a, b, (((ca,), (cb,)), ((), ())), preferred_element_type=F32)


def remote(src, dst, send, recv, where):
    return pltpu.make_async_remote_copy(
        src_ref=src,
        dst_ref=dst,
        send_sem=send,
        recv_sem=recv,
        device_id=where,
        device_id_type=pl.DeviceIdType.MESH,
    )


def arrived(ref, sem):
    pltpu.make_async_copy(ref, ref, sem).wait()


def kernel(
    geno,
    twice_freq,
    family_size,
    rel_family,
    rel_vector,
    rel_count,
    own_block,
    rel_block,
    prior,
    right_side,
    step_scale,
    out_solution,
    out_residual,
    words,
    codes,
    half_first,
    half_second,
    both,
    core_send,
    core_recv,
    chip_send,
    chip_recv,
    whole,
    total,
    gen_send,
    gen_recv,
    share_now,
    own_now,
    couple_now,
    right_now,
    rel_send,
    rel_first,
    rel_second,
    request,
    request_scalar,
    word_sem,
    local_sem,
    request_sem,
    core_sem,
    chip_sem,
    back_sem,
    join_sem,
    gen_sem,
    half_sem,
    rel_sem,
):
    animal = lax.axis_index("animal")
    snp = lax.axis_index("snp")
    core = lax.rem(animal, 2)
    chip = animal // 2
    partner = {"animal": animal + 1 - 2 * core}

    for block in range(ROW_BLOCKS):
        rows = pl.ds(block * (ROWS // ROW_BLOCKS), ROWS // ROW_BLOCKS)
        pltpu.make_async_copy(geno.at[rows], words.at[rows], word_sem.at[block]).start()
    family_first = snp * 2
    locals_ = [
        pltpu.make_async_copy(own_block.at[pl.ds(family_first, 2)], own_now, local_sem.at[0]),
        pltpu.make_async_copy(rel_block.at[pl.ds(family_first, 2)], couple_now, local_sem.at[1]),
        pltpu.make_async_copy(right_side.at[pl.ds(snp * SHARE, SHARE)], right_now, local_sem.at[2]),
    ]
    for copy in locals_:
        copy.start()
    halves = (half_first, half_second)
    rel_recv = (rel_first, rel_second)
    for ref in rel_recv:
        ref[...] = jnp.zeros_like(ref)

    barrier = pltpu.get_barrier_semaphore()
    for step in range(1, ANIMAL):
        pl.semaphore_signal(
            barrier,
            inc=1,
            device_id={"animal": lax.rem(animal + step, ANIMAL)},
            device_id_type=pl.DeviceIdType.MESH,
        )
    for step in range(1, SNP):
        pl.semaphore_signal(
            barrier,
            inc=1,
            device_id={"snp": lax.rem(snp + step, SNP)},
            device_id_type=pl.DeviceIdType.MESH,
        )

    lane_slot = lax.broadcasted_iota(jnp.int32, (COLS, FAM), 1)
    row_slot = lax.broadcasted_iota(jnp.int32, (FAM, COLS), 0)

    def first_half(f, carry):
        block = prior[pl.ds(pl.multiple_of(f * FAM, FAM), FAM), :]
        turned = block.astype(F32).T
        halves[0][f] = jnp.where(lane_slot < family_size[f], turned, 0.0).astype(BF16)
        return carry

    lax.fori_loop(0, FAMS, first_half, 0)
    live = [
        jnp.where(row_slot < family_size[family_first + i], 1.0, 0.0).astype(F32) for i in range(2)
    ]
    for i in range(2):
        block = prior[pl.ds(pl.multiple_of((family_first + i) * FAM, FAM), FAM), :]
        share_now[i] = live[i] * block.astype(F32)

    pl.semaphore_wait(barrier, ANIMAL - 1 + SNP - 1)

    for d in range(1, RSPAN + 1):

        @pl.when(animal >= d)
        def _():
            remote(
                rel_vector,
                request.at[d - 1],
                request_sem.at[0, d - 1],
                request_sem.at[1, d - 1],
                {"animal": animal - d},
            ).start()

    def decode_block(block, carry):
        rows = pl.ds(pl.multiple_of(block * (ROWS // ROW_BLOCKS), FAM), ROWS // ROW_BLOCKS)
        pltpu.make_async_copy(geno.at[rows], words.at[rows], word_sem.at[block]).wait()

        def decode(i, inner):
            at = pl.ds(pl.multiple_of(block * (ROWS // ROW_BLOCKS) + i * 16, 16), 16)
            word = words[at, :]
            for k in range(PLANES):
                codes[k, at, :] = ((word >> (2 * k)) & 3).astype(F32).astype(BF16)
            return inner

        return lax.fori_loop(0, ROWS // ROW_BLOCKS // 16, decode, carry)

    lax.fori_loop(0, ROW_BLOCKS, decode_block, 0)

    for d in range(1, RSPAN + 1):

        @pl.when(animal + d < ANIMAL)
        def _():
            arrived(request.at[d - 1], request_sem.at[1, d - 1])
            copy = pltpu.make_async_copy(
                request.at[d - 1], request_scalar.at[d - 1], local_sem.at[3]
            )
            copy.start()
            copy.wait()

    for copy in locals_:
        copy.wait()

    for it in range(ITERS):
        for d in range(1, RSPAN + 1):

            @pl.when(animal + d < ANIMAL)
            def _():
                for i in range(2):
                    wanted = lax.rem(request_scalar[d - 1, 0, family_first + i], FAMS)
                    rel_send[it, d - 1, i] = halves[it][wanted]
                remote(
                    rel_send.at[it, d - 1],
                    rel_recv[it].at[d - 1],
                    rel_sem.at[it, 0, d - 1],
                    rel_sem.at[it, 1, d - 1],
                    {"animal": animal + d},
                ).start()

        column_sum = jnp.zeros((COLS, FAM), F32)
        for f in range(FAMS):
            column_sum = column_sum + halves[it][f].astype(F32)
        column_sum = jnp.sum(column_sum, axis=1, keepdims=True)

        total[...] = jnp.zeros_like(total)

        def to_markers(k):
            turned = jnp.concatenate([halves[it][f] for f in range(FAMS)], axis=1)
            product = dot(turned, codes[k], 1, 0) - column_sum * twice_freq[k]
            both[k, 0] = product[:, :HALF]
            both[k, 1] = product[:, HALF:]
            core_send[it, k] = both[k, 1 - core].astype(BF16).reshape(CHIPS, BAND, HALF)
            remote(
                core_send.at[it, k],
                core_recv.at[it, k],
                core_sem.at[it, 0, k],
                core_sem.at[it, 1, k],
                partner,
            ).start()

        def over_chips(k):
            arrived(core_recv.at[it, k], core_sem.at[it, 1, k])
            summed = both[k, core].reshape(CHIPS, BAND, HALF) + core_recv[it, k].astype(F32)
            both[k, core] = summed.reshape(COLS, HALF)
            chip_send[it, k] = summed.astype(BF16)
            for d in range(1, CHIPS):
                to = lax.rem(chip + d, CHIPS)
                remote(
                    chip_send.at[it, k, to],
                    chip_recv.at[it, k, CHIPS - 1 - d],
                    chip_sem.at[it, 0, k],
                    chip_sem.at[it, 1, k],
                    {"animal": to * 2 + core},
                ).start()

        def to_chips(k):
            arrived(chip_recv.at[it, k], chip_sem.at[it, 1, k])
            mine = both[k, core, pl.ds(pl.multiple_of(chip * BAND, BAND), BAND), :]
            for d in range(CHIPS - 1):
                mine = mine + chip_recv[it, k, d].astype(F32)
            whole[it, k, core, chip] = mine.astype(BF16)
            for d in range(1, CHIPS):
                to = lax.rem(chip + d, CHIPS)
                remote(
                    whole.at[it, k, core, chip],
                    whole.at[it, k, core, chip],
                    back_sem.at[it, 0, k],
                    back_sem.at[it, 1, k],
                    {"animal": to * 2 + core},
                ).start()

        def to_core(k):
            arrived(chip_recv.at[it, k], back_sem.at[it, 1, k])
            remote(
                whole.at[it, k, core],
                whole.at[it, k, core],
                join_sem.at[it, 0, k],
                join_sem.at[it, 1, k],
                partner,
            ).start()

        def to_animals(k, shift):
            arrived(core_recv.at[it, k], join_sem.at[it, 1, k])
            lower = whole[it, k, 0].reshape(COLS, HALF)
            upper = whole[it, k, 1].reshape(COLS, HALF)
            sums = jnp.concatenate([lower, upper], axis=1)
            total[...] += dot(codes[k], sums, 1, 1)
            weighed = sums.astype(F32) * twice_freq[k]
            return shift + jnp.sum(weighed, axis=1, keepdims=True)

        def step(t, shift):
            for stage, offset in ((to_core, 3), (to_chips, 2), (over_chips, 1), (to_markers, 0)):
                k = t - offset

                @pl.when((k >= 0) & (k < PLANES))
                def _():
                    stage(k)

            k = t - 4
            return lax.cond(k >= 0, lambda s: to_animals(k, s), lambda s: s, shift)

        shift = lax.fori_loop(0, PLANES + 4, step, jnp.zeros((COLS, 1), F32))
        shift = jnp.broadcast_to(shift, (COLS, COLS)).T[:1]

        for d in range(1, SNP):
            to = lax.rem(snp + d, SNP)
            rows = pl.ds(pl.multiple_of(to * SHARE, SHARE), SHARE)
            gen_send[it, d - 1] = (total[rows, :] - shift).astype(BF16)
            remote(
                gen_send.at[it, d - 1],
                gen_recv.at[it, d - 1],
                gen_sem.at[it, 0],
                gen_sem.at[it, 1],
                {"snp": to},
            ).start()

        for d in range(1, RSPAN + 1):

            @pl.when(animal >= d)
            def _():
                arrived(rel_recv[it].at[d - 1], rel_sem.at[it, 1, d - 1])

        pedigree = []
        for i in range(2):
            family = family_first + i
            relative = rel_family[family]
            distance = animal - relative // FAMS
            here = halves[it][lax.rem(relative, FAMS)]
            there = rel_recv[it][jnp.clip(distance - 1, 0, RSPAN - 1), i]
            taken = jnp.where(distance == 0, here.astype(F32), there.astype(F32))
            taken = jnp.where(lane_slot < rel_count[family], taken, 0.0).astype(BF16)
            pedigree.append(
                dot(own_now[i], halves[it][family], 1, 1) + dot(couple_now[i], taken, 1, 1)
            )

        arrived(gen_recv.at[it], gen_sem.at[it, 1])
        for i in range(2):
            own_rows = pl.ds(pl.multiple_of(snp * SHARE + i * FAM, FAM), FAM)
            genomic = total[own_rows, :] - shift
            for d in range(SNP - 1):
                genomic = genomic + gen_recv[it, d, pl.ds(i * FAM, FAM), :].astype(F32)
            residual = live[i] * (
                right_now[pl.ds(i * FAM, FAM), :]
                - share_now[i]
                - GEN_WEIGHT / SNPS * genomic
                - pedigree[i]
            )
            scale = jnp.broadcast_to(step_scale[pl.ds(family_first + i, 1), :], (FAM, FAM)).T
            updated = share_now[i] + scale * residual
            if it + 1 < ITERS:
                share_now[i] = updated
                halves[it + 1][family_first + i] = updated.T.astype(BF16)
            else:
                out_solution[pl.ds(i * FAM, FAM), :] = updated
                out_residual[pl.ds(i * FAM, FAM), :] = residual

        if it + 1 < ITERS:
            mine = halves[it + 1].at[pl.ds(family_first, 2)]
            for d in range(1, SNP):
                remote(
                    mine,
                    mine,
                    half_sem.at[0],
                    half_sem.at[1],
                    {"snp": lax.rem(snp + d, SNP)},
                ).start()
            arrived(halves[it + 1].at[pl.ds(0, 14)], half_sem.at[1])

    arrived(halves[1].at[pl.ds(0, 14)], half_sem.at[0])
    for d in range(1, RSPAN + 1):

        @pl.when(animal >= d)
        def _():
            arrived(rel_vector, request_sem.at[0, d - 1])

        @pl.when(animal + d < ANIMAL)
        def _():
            for it in range(ITERS):
                arrived(rel_send.at[it, d - 1], rel_sem.at[it, 0, d - 1])

    for it in range(ITERS):
        arrived(gen_send.at[it], gen_sem.at[it, 0])

        def sent(k, carry):
            arrived(core_send.at[it, k], core_sem.at[it, 0, k])
            arrived(core_send.at[it, k], join_sem.at[it, 0, k])
            arrived(chip_recv.at[it, k], chip_sem.at[it, 0, k])
            arrived(chip_recv.at[it, k], back_sem.at[it, 0, k])
            return carry

        lax.fori_loop(0, PLANES, sent, 0)


def per_device(
    genotypes,
    allele_frequency,
    family_size,
    rel_family,
    rel_count,
    own_block,
    rel_block,
    prior_solution,
    right_side,
    step_scale,
):
    twice_freq = (2.0 * allele_frequency).reshape(WORDS, PLANES).T.reshape(PLANES, 1, WORDS)
    vmem = pl.BlockSpec(memory_space=pltpu.VMEM)
    smem = pl.BlockSpec(memory_space=pltpu.SMEM)
    hbm = pl.BlockSpec(memory_space=pl.ANY)
    dma = pltpu.SemaphoreType.DMA
    share = jax.ShapeDtypeStruct((SHARE, COLS), F32)
    rel_vector = jnp.pad(rel_family, (0, 128 - FAMS)).reshape(1, 128)
    return pl.pallas_call(
        kernel,
        out_shape=(share, share),
        in_specs=[hbm, vmem, smem, smem, vmem, smem, hbm, hbm, vmem, hbm, vmem],
        out_specs=(vmem, vmem),
        scratch_shapes=[
            pltpu.VMEM((ROWS, WORDS), jnp.int32),
            pltpu.VMEM((PLANES, ROWS, WORDS), BF16),
            pltpu.VMEM((FAMS, COLS, FAM), BF16),
            pltpu.VMEM((FAMS, COLS, FAM), BF16),
            pltpu.VMEM((PLANES, 2, COLS, HALF), F32),
            pltpu.VMEM((ITERS, PLANES, CHIPS, BAND, HALF), BF16),
            pltpu.VMEM((ITERS, PLANES, CHIPS, BAND, HALF), BF16),
            pltpu.VMEM((ITERS, PLANES, CHIPS, BAND, HALF), BF16),
            pltpu.VMEM((ITERS, PLANES, CHIPS - 1, BAND, HALF), BF16),
            pltpu.VMEM((ITERS, PLANES, 2, CHIPS, BAND, HALF), BF16),
            pltpu.VMEM((ROWS, COLS), F32),
            pltpu.VMEM((ITERS, SNP - 1, SHARE, COLS), BF16),
            pltpu.VMEM((ITERS, SNP - 1, SHARE, COLS), BF16),
            pltpu.VMEM((2, FAM, COLS), F32),
            pltpu.VMEM((2, FAM, FAM), BF16),
            pltpu.VMEM((2, FAM, FAM), BF16),
            pltpu.VMEM((SHARE, COLS), F32),
            pltpu.VMEM((ITERS, RSPAN, 2, COLS, FAM), BF16),
            pltpu.VMEM((RSPAN, 2, COLS, FAM), BF16),
            pltpu.VMEM((RSPAN, 2, COLS, FAM), BF16),
            pltpu.VMEM((RSPAN, 1, 128), jnp.int32),
            pltpu.SMEM((RSPAN, 1, 128), jnp.int32),
            dma((ROW_BLOCKS,)),
            dma((4,)),
            dma((2, RSPAN)),
            dma((ITERS, 2, PLANES)),
            dma((ITERS, 2, PLANES)),
            dma((ITERS, 2, PLANES)),
            dma((ITERS, 2, PLANES)),
            dma((ITERS, 2)),
            dma((2,)),
            dma((ITERS, 2, RSPAN)),
        ],
        compiler_params=pltpu.CompilerParams(
            collective_id=0, has_side_effects=True, vmem_limit_bytes=66 * 10**6
        ),
        name="blup",
    )(
        genotypes,
        twice_freq,
        family_size,
        rel_family,
        rel_vector,
        rel_count,
        own_block,
        rel_block,
        prior_solution,
        right_side,
        step_scale.reshape(FAMS, FAM),
    )


def solution(mesh):
    in_specs = (
        P("animal", "snp"),
        P("snp"),
        P("animal"),
        P("animal"),
        P("animal"),
        P("animal", None, None),
        P("animal", None, None),
        P("animal", None),
        P("animal", None),
        P("animal"),
    )
    out_specs = (P(("animal", "snp"), None), P(("animal", "snp"), None))
    return jax.shard_map(
        per_device, mesh=mesh, in_specs=in_specs, out_specs=out_specs, check_vma=False
    )
```

time: 515 us -> 133 us (0.26); the launches traced: 508 us -> 133 us
  blocking collectives: 182 us -> 0 us
  local copies, waits for them, and re-layouts: 184 us -> 5.6 us
  Pallas kernels: 0 us -> 126 us
  matrix products: 54.2 us -> 0 us
  other arithmetic: 47 us -> 0.74 us
  starting transfers between devices: 30.3 us -> 0 us
  waiting for transfers between devices: 8.87 us -> 0 us
    psum x2 -> x0, blocking collectives: 166 us -> none  [per_device(): snp_half = lax.psum(partial_sum, 'animal').astype(jnp.bfloat16)]
    pallas_call x0 -> x1, Pallas kernels: none -> 126 us  [per_device(): pl.pallas_call(kernel, out_shape=(share, share), in_specs=[hbm, vmem, sme...]
    shift_right_arithmetic x16 -> x0, local copies, waits for them, and re-layouts: 96 us -> none  [decode_rows(): jnp.right_shift(genotypes[:, :, None], bit_shifts[None, None, :])]
    dynamic_update_slice x8 -> x0, local copies, waits for them, and re-layouts: 59.4 us -> none  [decode_blocks(): decoded = lax.map(decode_group, (packed_marker_groups, live_groups))]
    dot_general x8 -> x0, matrix products: 54.2 us -> none  [the longest x2 26.3 us: per_device(): lax.dot_general(centered, solution_half, (((0,), (0,)), ((), ())), prefer...]
    convert_element_type x7 -> x0, other arithmetic: 36.6 us -> none  [the longest x4 34.7 us: decode_rows(): return centered.astype(jnp.bfloat16)]
    dynamic_slice x17 -> x0, local copies, waits for them, and re-layouts: 22.9 us -> none  [the longest x12 20.5 us: decode_blocks(): decoded = lax.map(decode_group, (packed_marker_groups, live_groups))]
    ppermute x6 -> x0, starting transfers between devices: 20.1 us -> none  [shifted(): return lax.ppermute(array, axis, pairs)]
  transfers between devices with their start and end apart: 8 -> 0, of which waited for: 2 -> 0; matrix products, arithmetic and copies ran while one was open for 52% -> 0% of each run, Pallas kernels for 0% -> 0%
where the time goes in v1:
time: 133 us
  Pallas kernels  126 us (95%)
  local copies, waits for them, and re-layouts  5.6 us (4%)
    pallas_call x1, Pallas kernels, per_device(): pl.pallas_call(kernel, out_shape=(share, share), in_specs=[hbm, vmem, sme...  126 us
    unnamed x2, local copies, waits for them, and re-layouts  3.14 us

profile of v1, /device:TPU:1, one launch (start us, length us, event | category | flops | bytes accessed | tf_op | source)
XLA Modules:
  0.0 133.0 jit_solution(4037073344847740786)
XLA Ops:
  0.6 0.7 broadcast_multiply_fusion
  1.4 0.5 reshape.16
  1.9 0.2 copy.12
  2.0 0.6 reshape.17.twice_freq
  2.7 1.2 pad_bitcast_fusion.rel_vector
  3.8 126.0 %blup.1 = (f32[256,128]{1,0:T(8,128)}, f32[256,128]{1,0:T(8,128)}) custom-call(s32[2048,1024]{1,0:T(8,128)} %geno.1, f32[6,1,1024]{2,1,0:T(1,128)} %reshape.17.twice_freq, s32[16]{0:T(128)} %family_size.1, s32[16]{0:T(128)} %rel_family.1, s32[1,128]{1,0:T(1,128)} %pad_bitcast_fusion.rel_vector, s32[16]{0:T(128)} %rel_count.1, ...), custom_call_target="tpu_custom_call" | custom-call | tf_op jit(solution)/shard_map/blup/pallas_call | solution.py:403
  129.8 1.6 %copy.15 = f32[256,128]{1,0:T(8,128)} copy(f32[256,128]{1,0:T(8,128)} %get-tuple-element.4) | data formatting | bytes 262144
  131.4 1.6 %copy.16 = f32[256,128]{1,0:T(8,128)} copy(f32[256,128]{1,0:T(8,128)} %get-tuple-element.5) | data formatting | bytes 262144

commit v2 on v1

--- a/solution.py
+++ b/solution.py
@@ -48,7 +48,7 @@
 
 def kernel(
     geno,
-    twice_freq,
+    freq,
     family_size,
     rel_family,
     rel_vector,
@@ -58,8 +58,7 @@
     prior,
     right_side,
     step_scale,
-    out_solution,
-    out_residual,
+    out,
     words,
     codes,
     half_first,
@@ -80,8 +79,13 @@
     rel_send,
     rel_first,
     rel_second,
-    request,
-    request_scalar,
+    request_one,
+    request_two,
+    request_three,
+    scalar_one,
+    scalar_two,
+    scalar_three,
+    twice_freq,
     word_sem,
     local_sem,
     request_sem,
@@ -97,7 +101,18 @@
     snp = lax.axis_index("snp")
     core = lax.rem(animal, 2)
     chip = animal // 2
+    request = (request_one, request_two, request_three)
+    request_scalar = (scalar_one, scalar_two, scalar_three)
     partner = {"animal": animal + 1 - 2 * core}
+    other_chips = [
+        lax.rem(chip // 2 + dz, 4) * 2 + lax.rem(lax.rem(chip, 2) + dx, 2)
+        for dz, dx in ((2, 1), (1, 1), (3, 1), (2, 0), (1, 0), (3, 0), (0, 1))
+    ]
+
+    def peer(step):
+        far = 1 - step // 4
+        return lax.rem(snp // 4 + far, 2) * 4 + lax.rem(lax.rem(snp, 4) + 3 - lax.rem(step, 4), 4)
+
 
     for block in range(ROW_BLOCKS):
         rows = pl.ds(block * (ROWS // ROW_BLOCKS), ROWS // ROW_BLOCKS)
@@ -148,65 +163,43 @@
         block = prior[pl.ds(pl.multiple_of((family_first + i) * FAM, FAM), FAM), :]
         share_now[i] = live[i] * block.astype(F32)
 
-    pl.semaphore_wait(barrier, ANIMAL - 1 + SNP - 1)
-
-    for d in range(1, RSPAN + 1):
-
-        @pl.when(animal >= d)
-        def _():
-            remote(
-                rel_vector,
-                request.at[d - 1],
-                request_sem.at[0, d - 1],
-                request_sem.at[1, d - 1],
-                {"animal": animal - d},
-            ).start()
+    lane = lax.broadcasted_iota(jnp.int32, (128, PLANES * 128), 0)
+    column = lax.broadcasted_iota(jnp.int32, (128, PLANES * 128), 1)
+    marker = PLANES * (column & 127) + (column >> 7)
+    by_plane = jnp.zeros((24, PLANES * 128), F32)
+    for r in range(PLANES):
+        rest = 2.0 * freq[pl.ds(r, 8, stride=PLANES), :]
+        parts = []
+        for _ in range(3):
+            part = rest.astype(BF16).astype(F32)
+            parts.append(part)
+            rest = rest - part
+        chosen = jnp.where(marker == lane + 128 * r, 1.0, 0.0).astype(BF16)
+        by_plane = by_plane + dot(jnp.concatenate(parts, axis=0).astype(BF16), chosen, 1, 0)
+    by_plane = by_plane[:8] + by_plane[8:16] + by_plane[16:]
+    for k in range(PLANES):
+        for q in range(8):
+            twice_freq[k, :, pl.ds(q * 128, 128)] = by_plane[q : q + 1, k * 128 : (k + 1) * 128]
 
     def decode_block(block, carry):
-        rows = pl.ds(pl.multiple_of(block * (ROWS // ROW_BLOCKS), FAM), ROWS // ROW_BLOCKS)
+        size = ROWS // ROW_BLOCKS
+        rows = pl.ds(pl.multiple_of(block * size, size), size)
         pltpu.make_async_copy(geno.at[rows], words.at[rows], word_sem.at[block]).wait()
-
         def decode(i, inner):
-            at = pl.ds(pl.multiple_of(block * (ROWS // ROW_BLOCKS) + i * 16, 16), 16)
+            at = pl.ds(pl.multiple_of(block * size + i * 16, 16), 16)
             word = words[at, :]
             for k in range(PLANES):
                 codes[k, at, :] = ((word >> (2 * k)) & 3).astype(F32).astype(BF16)
             return inner
 
-        return lax.fori_loop(0, ROWS // ROW_BLOCKS // 16, decode, carry)
+        return lax.fori_loop(0, size // 16, decode, carry)
 
     lax.fori_loop(0, ROW_BLOCKS, decode_block, 0)
-
-    for d in range(1, RSPAN + 1):
-
-        @pl.when(animal + d < ANIMAL)
-        def _():
-            arrived(request.at[d - 1], request_sem.at[1, d - 1])
-            copy = pltpu.make_async_copy(
-                request.at[d - 1], request_scalar.at[d - 1], local_sem.at[3]
-            )
-            copy.start()
-            copy.wait()
 
     for copy in locals_:
         copy.wait()
 
     for it in range(ITERS):
-        for d in range(1, RSPAN + 1):
-
-            @pl.when(animal + d < ANIMAL)
-            def _():
-                for i in range(2):
-                    wanted = lax.rem(request_scalar[d - 1, 0, family_first + i], FAMS)
-                    rel_send[it, d - 1, i] = halves[it][wanted]
-                remote(
-                    rel_send.at[it, d - 1],
-                    rel_recv[it].at[d - 1],
-                    rel_sem.at[it, 0, d - 1],
-                    rel_sem.at[it, 1, d - 1],
-                    {"animal": animal + d},
-                ).start()
-
         column_sum = jnp.zeros((COLS, FAM), F32)
         for f in range(FAMS):
             column_sum = column_sum + halves[it][f].astype(F32)
@@ -220,6 +213,8 @@
             both[k, 0] = product[:, :HALF]
             both[k, 1] = product[:, HALF:]
             core_send[it, k] = both[k, 1 - core].astype(BF16).reshape(CHIPS, BAND, HALF)
+
+        def send_core(k):
             remote(
                 core_send.at[it, k],
                 core_recv.at[it, k],
@@ -233,11 +228,10 @@
             summed = both[k, core].reshape(CHIPS, BAND, HALF) + core_recv[it, k].astype(F32)
             both[k, core] = summed.reshape(COLS, HALF)
             chip_send[it, k] = summed.astype(BF16)
-            for d in range(1, CHIPS):
-                to = lax.rem(chip + d, CHIPS)
+            for slot, to in enumerate(other_chips):
                 remote(
                     chip_send.at[it, k, to],
-                    chip_recv.at[it, k, CHIPS - 1 - d],
+                    chip_recv.at[it, k, slot],
                     chip_sem.at[it, 0, k],
                     chip_sem.at[it, 1, k],
                     {"animal": to * 2 + core},
@@ -249,8 +243,7 @@
             for d in range(CHIPS - 1):
                 mine = mine + chip_recv[it, k, d].astype(F32)
             whole[it, k, core, chip] = mine.astype(BF16)
-            for d in range(1, CHIPS):
-                to = lax.rem(chip + d, CHIPS)
+            for to in other_chips:
                 remote(
                     whole.at[it, k, core, chip],
                     whole.at[it, k, core, chip],
@@ -269,40 +262,113 @@
                 partner,
             ).start()
 
-        def to_animals(k, shift):
+        def marker_sums(k):
             arrived(core_recv.at[it, k], join_sem.at[it, 1, k])
             lower = whole[it, k, 0].reshape(COLS, HALF)
             upper = whole[it, k, 1].reshape(COLS, HALF)
             sums = jnp.concatenate([lower, upper], axis=1)
+            weighed = sums.astype(F32) * twice_freq[k]
+            return sums, jnp.sum(weighed, axis=1, keepdims=True)
+
+        def to_animals(k, shift):
+            sums, weighed = marker_sums(k)
             total[...] += dot(codes[k], sums, 1, 1)
-            weighed = sums.astype(F32) * twice_freq[k]
-            return shift + jnp.sum(weighed, axis=1, keepdims=True)
-
-        def step(t, shift):
-            for stage, offset in ((to_core, 3), (to_chips, 2), (over_chips, 1), (to_markers, 0)):
-                k = t - offset
-
-                @pl.when((k >= 0) & (k < PLANES))
+            return shift + weighed
+
+        def out_step(t, carry):
+            to_markers(t)
+            send_core(t)
+            over_chips(t - 1)
+            return carry
+
+        to_markers(0)
+        if it == 0:
+                pl.semaphore_wait(barrier, ANIMAL - 1 + SNP - 1)
+
+                for d in range(1, RSPAN + 1):
+
+                    @pl.when(animal >= d)
+                    def _():
+                        remote(
+                            rel_vector,
+                            request[d - 1],
+                            request_sem.at[0, d - 1],
+                            request_sem.at[1, d - 1],
+                            {"animal": animal - d},
+                        ).start()
+
+
+        send_core(0)
+        lax.fori_loop(1, PLANES, out_step, 0)
+        over_chips(PLANES - 1)
+
+        def back_step(k, carry):
+            to_chips(k)
+            return carry
+
+        lax.fori_loop(0, PLANES, back_step, 0)
+
+        if it == 0:
+
+            for d in range(1, RSPAN + 1):
+
+                @pl.when(animal + d < ANIMAL)
                 def _():
-                    stage(k)
-
-            k = t - 4
-            return lax.cond(k >= 0, lambda s: to_animals(k, s), lambda s: s, shift)
-
-        shift = lax.fori_loop(0, PLANES + 4, step, jnp.zeros((COLS, 1), F32))
-        shift = jnp.broadcast_to(shift, (COLS, COLS)).T[:1]
-
-        for d in range(1, SNP):
-            to = lax.rem(snp + d, SNP)
+                    arrived(request[d - 1], request_sem.at[1, d - 1])
+                    copy = pltpu.make_async_copy(
+                        request[d - 1], request_scalar[d - 1], local_sem.at[3]
+                    )
+                    copy.start()
+                    copy.wait()
+
+        for d in range(1, RSPAN + 1):
+
+            @pl.when(animal + d < ANIMAL)
+            def _():
+                for i in range(2):
+                    wanted = lax.rem(request_scalar[d - 1][family_first + i], FAMS)
+                    rel_send[it, d - 1, i] = halves[it][wanted]
+                remote(
+                    rel_send.at[it, d - 1],
+                    rel_recv[it].at[d - 1],
+                    rel_sem.at[it, 0, d - 1],
+                    rel_sem.at[it, 1, d - 1],
+                    {"animal": animal + d},
+                ).start()
+
+        to_core(0)
+
+        def in_step(k, shift):
+            to_core(k)
+            return to_animals(k - 1, shift)
+
+        shift = lax.fori_loop(1, PLANES, in_step, jnp.zeros((COLS, 1), F32))
+        sums, weighed = marker_sums(PLANES - 1)
+        shift = jnp.broadcast_to(shift + weighed, (COLS, COLS)).T[:1]
+
+        def last_block(d, carry):
+            to = peer(d)
             rows = pl.ds(pl.multiple_of(to * SHARE, SHARE), SHARE)
-            gen_send[it, d - 1] = (total[rows, :] - shift).astype(BF16)
-            remote(
-                gen_send.at[it, d - 1],
-                gen_recv.at[it, d - 1],
-                gen_sem.at[it, 0],
-                gen_sem.at[it, 1],
-                {"snp": to},
-            ).start()
+            block = total[rows, :] - shift + dot(codes[PLANES - 1, rows, :], sums, 1, 1)
+
+            @pl.when(d < SNP - 1)
+            def _():
+                gen_send[it, d] = block.astype(BF16)
+                remote(
+                    gen_send.at[it, d],
+                    gen_recv.at[it, d],
+                    gen_sem.at[it, 0],
+                    gen_sem.at[it, 1],
+                    {"snp": to},
+                ).start()
+
+            @pl.when(d == SNP - 1)
+            def _():
+                total[rows, :] = block
+
+            return carry
+
+        lax.fori_loop(0, SNP, last_block, 0)
 
         for d in range(1, RSPAN + 1):
 
@@ -326,7 +392,7 @@
         arrived(gen_recv.at[it], gen_sem.at[it, 1])
         for i in range(2):
             own_rows = pl.ds(pl.multiple_of(snp * SHARE + i * FAM, FAM), FAM)
-            genomic = total[own_rows, :] - shift
+            genomic = total[own_rows, :]
             for d in range(SNP - 1):
                 genomic = genomic + gen_recv[it, d, pl.ds(i * FAM, FAM), :].astype(F32)
             residual = live[i] * (
@@ -341,18 +407,18 @@
                 share_now[i] = updated
                 halves[it + 1][family_first + i] = updated.T.astype(BF16)
             else:
-                out_solution[pl.ds(i * FAM, FAM), :] = updated
-                out_residual[pl.ds(i * FAM, FAM), :] = residual
+                out[0, pl.ds(i * FAM, FAM), :] = updated
+                out[1, pl.ds(i * FAM, FAM), :] = residual
 
         if it + 1 < ITERS:
             mine = halves[it + 1].at[pl.ds(family_first, 2)]
-            for d in range(1, SNP):
+            for d in range(SNP - 1):
                 remote(
                     mine,
                     mine,
                     half_sem.at[0],
                     half_sem.at[1],
-                    {"snp": lax.rem(snp + d, SNP)},
+                    {"snp": peer(d)},
                 ).start()
             arrived(halves[it + 1].at[pl.ds(0, 14)], half_sem.at[1])
 
@@ -393,18 +459,15 @@
     right_side,
     step_scale,
 ):
-    twice_freq = (2.0 * allele_frequency).reshape(WORDS, PLANES).T.reshape(PLANES, 1, WORDS)
     vmem = pl.BlockSpec(memory_space=pltpu.VMEM)
     smem = pl.BlockSpec(memory_space=pltpu.SMEM)
     hbm = pl.BlockSpec(memory_space=pl.ANY)
     dma = pltpu.SemaphoreType.DMA
-    share = jax.ShapeDtypeStruct((SHARE, COLS), F32)
-    rel_vector = jnp.pad(rel_family, (0, 128 - FAMS)).reshape(1, 128)
-    return pl.pallas_call(
+    both = pl.pallas_call(
         kernel,
-        out_shape=(share, share),
+        out_shape=jax.ShapeDtypeStruct((2, SHARE, COLS), F32),
         in_specs=[hbm, vmem, smem, smem, vmem, smem, hbm, hbm, vmem, hbm, vmem],
-        out_specs=(vmem, vmem),
+        out_specs=vmem,
         scratch_shapes=[
             pltpu.VMEM((ROWS, WORDS), jnp.int32),
             pltpu.VMEM((PLANES, ROWS, WORDS), BF16),
@@ -426,8 +489,9 @@
             pltpu.VMEM((ITERS, RSPAN, 2, COLS, FAM), BF16),
             pltpu.VMEM((RSPAN, 2, COLS, FAM), BF16),
             pltpu.VMEM((RSPAN, 2, COLS, FAM), BF16),
-            pltpu.VMEM((RSPAN, 1, 128), jnp.int32),
-            pltpu.SMEM((RSPAN, 1, 128), jnp.int32),
+            *[pltpu.VMEM((FAMS,), jnp.int32)] * RSPAN,
+            *[pltpu.SMEM((FAMS,), jnp.int32)] * RSPAN,
+            pltpu.VMEM((PLANES, 1, WORDS), F32),
             dma((ROW_BLOCKS,)),
             dma((4,)),
             dma((2, RSPAN)),
@@ -445,10 +509,10 @@
         name="blup",
     )(
         genotypes,
-        twice_freq,
+        allele_frequency.reshape(PLANES * WORDS // 128, 128),
         family_size,
         rel_family,
-        rel_vector,
+        rel_family,
         rel_count,
         own_block,
         rel_block,
@@ -456,6 +520,7 @@
         right_side,
         step_scale.reshape(FAMS, FAM),
     )
+    return both[0], both[1]
 
 
 def solution(mesh):

time: 133 us -> 93.9 us (0.71)
  Pallas kernels: 126 us -> 91.4 us
  local copies, waits for them, and re-layouts: 5.6 us -> 1.69 us
    pallas_call x1, Pallas kernels: 126 us -> 91.4 us  [per_device(): pl.pallas_call(kernel, out_shape=jax.ShapeDtypeStruct((2, SHARE, COLS), F...]
    unnamed x2 -> x0, local copies, waits for them, and re-layouts: 3.14 us -> none
    reshape x4 -> x0, local copies, waits for them, and re-layouts: 2.47 us -> none  [the longest x3 1.3 us: per_device(): (2.0 * allele_frequency).reshape(WORDS, PLANES).T.reshape(PLANES, 1, WORDS)]
    squeeze x0 -> x1, local copies, waits for them, and re-layouts: none -> 1.69 us  [per_device(): return (both[0], both[1])]
where the time goes in v2:
time: 93.9 us; the launch traced here: 93.7 us
  Pallas kernels  91.4 us (97%)
  local copies, waits for them, and re-layouts  1.69 us (2%)
    pallas_call x1, Pallas kernels, per_device(): pl.pallas_call(kernel, out_shape=jax.ShapeDtypeStruct((2, SHARE, COLS), F...  91.4 us

profile of v2, /device:TPU:1, one launch (start us, length us, event | category | flops | bytes accessed | tf_op | source)
XLA Modules:
  0.0 93.7 jit_solution(16843985098366379383)
XLA Ops:
  0.6 91.4 %blup.1 = f32[2,256,128]{2,1,0:T(8,128)} custom-call(s32[2048,1024]{1,0:T(8,128)} %geno.1, f32[48,128]{1,0:T(8,128)} %bitcast.6, s32[16]{0:T(128)} %family_size.1, s32[16]{0:T(128)} %rel_vector.1, s32[16]{0:T(128)} %rel_vector.1, s32[16]{0:T(128)} %rel_count.1, bf16[16,128,128]{2,1,0:T(8,128)(2,1)} %own_block.1, bf16[16,128,128]{2,1,0:T(8,128)(2,1)} %rel_block.1, ...), custom_call_target="tpu_custom_call" | custom-call | tf_op jit(solution)/shard_map/blup/pallas_call | solution.py:466
  92.1 1.7 %slice_bitcast_fusion = (f32[256,128]{1,0:T(8,128)}, f32[256,128]{1,0:T(8,128)}) fusion(f32[2,256,128]{2,1,0:T(8,128)} %blup.1), kind=kLoop, calls=%fused_computation | loop fusion | bytes 524288 | tf_op jit(solution)/shard_map/squeeze | solution.py:523

commit v3 on v2

--- a/solution.py
+++ b/solution.py
@@ -10,6 +10,7 @@
 RSPAN = 3
 GEN_WEIGHT = 6.0
 PLANES = 6
+EARLY = 3
 FAM = 128
 COLS = 128
 ANIMAL = 16
@@ -25,6 +26,7 @@
 
 F32 = jnp.float32
 BF16 = jnp.bfloat16
+F8 = jnp.float8_e4m3fn
 
 
 def dot(a, b, ca, cb):
@@ -186,18 +188,26 @@
         rows = pl.ds(pl.multiple_of(block * size, size), size)
         pltpu.make_async_copy(geno.at[rows], words.at[rows], word_sem.at[block]).wait()
         def decode(i, inner):
-            at = pl.ds(pl.multiple_of(block * size + i * 16, 16), 16)
+            at = pl.ds(pl.multiple_of(block * size + i * 32, 32), 32)
             word = words[at, :]
-            for k in range(PLANES):
-                codes[k, at, :] = ((word >> (2 * k)) & 3).astype(F32).astype(BF16)
+            for k in range(EARLY):
+                codes[k, at, :] = ((word >> (2 * k)) & 3).astype(F32).astype(F8)
             return inner
 
-        return lax.fori_loop(0, size // 16, decode, carry)
+        return lax.fori_loop(0, size // 32, decode, carry)
 
     lax.fori_loop(0, ROW_BLOCKS, decode_block, 0)
 
     for copy in locals_:
         copy.wait()
+
+    def decode_plane(k):
+        def decode(i, carry):
+            at = pl.ds(pl.multiple_of(i * 128, 128), 128)
+            codes[k, at, :] = ((words[at, :] >> (2 * k)) & 3).astype(F32).astype(F8)
+            return carry
+
+        lax.fori_loop(0, ROWS // 128, decode, 0)
 
     for it in range(ITERS):
         column_sum = jnp.zeros((COLS, FAM), F32)
@@ -267,15 +277,31 @@
             lower = whole[it, k, 0].reshape(COLS, HALF)
             upper = whole[it, k, 1].reshape(COLS, HALF)
             sums = jnp.concatenate([lower, upper], axis=1)
-            weighed = sums.astype(F32) * twice_freq[k]
-            return sums, jnp.sum(weighed, axis=1, keepdims=True)
+            sums = sums.astype(F32)
+            weighed = jnp.sum(sums * twice_freq[k], axis=1, keepdims=True)
+            largest = jnp.max(jnp.max(jnp.abs(sums), axis=1, keepdims=True), axis=0, keepdims=True)
+            unit = jnp.maximum(largest, 1e-30) * (1 / 224)
+            scaled = sums * (1 / unit)
+            high = scaled.astype(F8)
+            low = ((scaled - high.astype(F32)) * 16).astype(F8)
+            return jnp.concatenate([high, low], axis=0), unit, weighed
+
+        def animal_product(rows_codes, sums, unit):
+            pair = dot(rows_codes, sums, 1, 1)
+            return (pair[:, :COLS] + pair[:, COLS:] * (1 / 16)) * unit
 
         def to_animals(k, shift):
-            sums, weighed = marker_sums(k)
-            total[...] += dot(codes[k], sums, 1, 1)
+            sums, unit, weighed = marker_sums(k)
+            total[...] += animal_product(codes[k], sums, unit)
             return shift + weighed
 
         def out_step(t, carry):
+            if it == 0:
+
+                @pl.when(t >= EARLY)
+                def _():
+                    decode_plane(t)
+
             to_markers(t)
             send_core(t)
             over_chips(t - 1)
@@ -343,13 +369,14 @@
             return to_animals(k - 1, shift)
 
         shift = lax.fori_loop(1, PLANES, in_step, jnp.zeros((COLS, 1), F32))
-        sums, weighed = marker_sums(PLANES - 1)
+        sums, unit, weighed = marker_sums(PLANES - 1)
         shift = jnp.broadcast_to(shift + weighed, (COLS, COLS)).T[:1]
 
         def last_block(d, carry):
             to = peer(d)
             rows = pl.ds(pl.multiple_of(to * SHARE, SHARE), SHARE)
-            block = total[rows, :] - shift + dot(codes[PLANES - 1, rows, :], sums, 1, 1)
+            part = animal_product(codes[PLANES - 1, rows, :], sums, unit)
+            block = total[rows, :] - shift + part
 
             @pl.when(d < SNP - 1)
             def _():
@@ -470,7 +497,7 @@
         out_specs=vmem,
         scratch_shapes=[
             pltpu.VMEM((ROWS, WORDS), jnp.int32),
-            pltpu.VMEM((PLANES, ROWS, WORDS), BF16),
+            pltpu.VMEM((PLANES, ROWS, WORDS), F8),
             pltpu.VMEM((FAMS, COLS, FAM), BF16),
             pltpu.VMEM((FAMS, COLS, FAM), BF16),
             pltpu.VMEM((PLANES, 2, COLS, HALF), F32),

time: 93.9 us -> 91.1 us (0.970)
  Pallas kernels: 91.4 us -> 88.6 us
    pallas_call x1, Pallas kernels: 91.4 us -> 88.6 us  [per_device(): pl.pallas_call(kernel, out_shape=jax.ShapeDtypeStruct((2, SHARE, COLS), F...]
where the time goes in v3:
time: 91.1 us; the launch traced here: 90.9 us
  Pallas kernels  88.6 us (97%)
  local copies, waits for them, and re-layouts  1.69 us (2%)
    pallas_call x1, Pallas kernels, per_device(): pl.pallas_call(kernel, out_shape=jax.ShapeDtypeStruct((2, SHARE, COLS), F...  88.6 us

profile of v3, /device:TPU:1, one launch (start us, length us, event | category | flops | bytes accessed | tf_op | source)
XLA Modules:
  0.0 90.9 jit_solution(6789335342743336931)
XLA Ops:
  0.6 88.6 %blup.1 = f32[2,256,128]{2,1,0:T(8,128)} custom-call(s32[2048,1024]{1,0:T(8,128)} %geno.1, f32[48,128]{1,0:T(8,128)} %bitcast.6, s32[16]{0:T(128)} %family_size.1, s32[16]{0:T(128)} %rel_vector.1, s32[16]{0:T(128)} %rel_vector.1, s32[16]{0:T(128)} %rel_count.1, bf16[16,128,128]{2,1,0:T(8,128)(2,1)} %own_block.1, bf16[16,128,128]{2,1,0:T(8,128)(2,1)} %rel_block.1, ...), custom_call_target="tpu_custom_call" | custom-call | tf_op jit(solution)/shard_map/blup/pallas_call | solution.py:493
  89.3 1.7 %slice_bitcast_fusion = (f32[256,128]{1,0:T(8,128)}, f32[256,128]{1,0:T(8,128)}) fusion(f32[2,256,128]{2,1,0:T(8,128)} %blup.1), kind=kLoop, calls=%fused_computation | loop fusion | bytes 524288 | tf_op jit(solution)/shard_map/squeeze | solution.py:550

commit v4 on v3

--- a/solution.py
+++ b/solution.py
@@ -278,12 +278,13 @@
             upper = whole[it, k, 1].reshape(COLS, HALF)
             sums = jnp.concatenate([lower, upper], axis=1)
             sums = sums.astype(F32)
-            weighed = jnp.sum(sums * twice_freq[k], axis=1, keepdims=True)
             largest = jnp.max(jnp.max(jnp.abs(sums), axis=1, keepdims=True), axis=0, keepdims=True)
             unit = jnp.maximum(largest, 1e-30) * (1 / 224)
             scaled = sums * (1 / unit)
             high = scaled.astype(F8)
             low = ((scaled - high.astype(F32)) * 16).astype(F8)
+            kept = high.astype(F32) + low.astype(F32) * (1 / 16)
+            weighed = jnp.sum(kept * twice_freq[k], axis=1, keepdims=True) * unit
             return jnp.concatenate([high, low], axis=0), unit, weighed
 
         def animal_product(rows_codes, sums, unit):

time: 91.1 us -> 91.4 us (level)
  no operation moved by 1% of the time
where the time goes in v4:
time: 91.4 us; the launch traced here: 91.3 us
  Pallas kernels  88.9 us (97%)
  local copies, waits for them, and re-layouts  1.69 us (2%)
    pallas_call x1, Pallas kernels, per_device(): pl.pallas_call(kernel, out_shape=jax.ShapeDtypeStruct((2, SHARE, COLS), F...  88.9 us

profile of v4, /device:TPU:1, one launch (start us, length us, event | category | flops | bytes accessed | tf_op | source)
XLA Modules:
  0.0 91.3 jit_solution(17190325396672722807)
XLA Ops:
  0.6 88.9 %blup.1 = f32[2,256,128]{2,1,0:T(8,128)} custom-call(s32[2048,1024]{1,0:T(8,128)} %geno.1, f32[48,128]{1,0:T(8,128)} %bitcast.6, s32[16]{0:T(128)} %family_size.1, s32[16]{0:T(128)} %rel_vector.1, s32[16]{0:T(128)} %rel_vector.1, s32[16]{0:T(128)} %rel_count.1, bf16[16,128,128]{2,1,0:T(8,128)(2,1)} %own_block.1, bf16[16,128,128]{2,1,0:T(8,128)(2,1)} %rel_block.1, ...), custom_call_target="tpu_custom_call" | custom-call | tf_op jit(solution)/shard_map/blup/pallas_call | solution.py:494
  89.6 1.7 %slice_bitcast_fusion = (f32[256,128]{1,0:T(8,128)}, f32[256,128]{1,0:T(8,128)}) fusion(f32[2,256,128]{2,1,0:T(8,128)} %blup.1), kind=kLoop, calls=%fused_computation | loop fusion | bytes 524288 | tf_op jit(solution)/shard_map/squeeze | solution.py:551
